TPU v7x, 32 devices: a whole 2x2x4 slice. The times are simulated.
32 devices in a mesh: grp: 4 (over y, x), gx: 4 (over z), gy: 2 (over core).
Axes of the slice: x: 2, y: 2, z: 4, core: 2. Of those that a mesh axis runs over, the one named last changes fastest.
Arguments:
- coarse_modes: float32 [4, 2, 8, 32, 4096], P('grp', None, None, 'gy', 'gx'), may hold values from -6 to 6
- salinity: float32 [32, 128, 16384], P('grp', 'gy', 'gx'), may hold values from -6 to 6
- viscosity: float32 [4], P('grp'), may hold values from 0.1 to 1
- forcing_gain: float32 [4], P('grp'), may hold values from 0.5 to 2
- diffusivity: float32 [32], P('grp'), may hold values from 0.3 to 1.5
Outputs:
- salinity_next: float32 [32, 128, 16384], P('grp', 'gy', 'gx')
- coarse_next: float32 [4, 2, 8, 32, 4096], P('grp', None, None, 'gy', 'gx')
All inputs are finite; a program needn't handle non-finite values.
Results may differ from a plain program's by a relative error of at most 0.0003.
Values sent between devices are 32-bit elements; how exact they have to be, the bound alone decides.
A program may use at most 192 MiB of HBM per device.

v0:
```python
import math
import jax
import jax.numpy as jnp
from jax import lax
from jax.sharding import PartitionSpec as P

RATIO = 4
fine_step = 0.1


def extended(cells, sides, width):
    for axis, dim in sides:
        count = lax.axis_size(axis)
        head = lax.slice_in_dim(cells, 0, width, axis=dim)
        tail = lax.slice_in_dim(cells, cells.shape[dim] - width, cells.shape[dim], axis=dim)
        cells = jnp.concatenate(
            [
                lax.ppermute(tail, axis, [(i, (i + 1) % count) for i in range(count)]),
                cells,
                lax.ppermute(head, axis, [((i + 1) % count, i) for i in range(count)]),
            ],
            axis=dim,
        )
    return cells


def circle_table(row_count, col_count, period, orient):
    product = (
        lax.broadcasted_iota(jnp.int32, (row_count, col_count), 0)
        * lax.broadcasted_iota(jnp.int32, (row_count, col_count), 1)
        % period
    )
    angle = 2.0 * math.pi / period * product.astype(jnp.float32)
    return (jnp.cos(angle), orient * jnp.sin(angle))


def contract(data, table, form):
    return jnp.einsum(form, data, table, precision=lax.Precision.HIGHEST)


def fourier_lines(real_part, imag_part, orient, want_imag):
    length = real_part.shape[-1]
    exponent = length.bit_length() - 1
    inner_count = 2 ** ((exponent + 2) // 2)
    outer_count = length // inner_count
    leading = real_part.shape[:-1]
    cos_outer, sin_outer = circle_table(outer_count, outer_count, outer_count, orient)
    cos_twist, sin_twist = circle_table(outer_count, inner_count, length, orient)
    cos_inner, sin_inner = circle_table(inner_count, inner_count, inner_count, orient)
    first_form = "...ba,bk->...ka"
    second_form = "...ka,aj->...jk"
    split_real = real_part.reshape(leading + (outer_count, inner_count))
    section_real = contract(split_real, cos_outer, first_form)
    section_imag = contract(split_real, sin_outer, first_form)
    if imag_part is not None:
        split_imag = imag_part.reshape(leading + (outer_count, inner_count))
        section_real = section_real - contract(split_imag, sin_outer, first_form)
        section_imag = section_imag + contract(split_imag, cos_outer, first_form)
    twist_real = section_real * cos_twist - section_imag * sin_twist
    twist_imag = section_real * sin_twist + section_imag * cos_twist
    norm_factor = length ** (-0.5)
    final_real = (
        contract(twist_real, cos_inner, second_form) - contract(twist_imag, sin_inner, second_form)
    ) * norm_factor
    if not want_imag:
        return final_real.reshape(leading + (length,))
    final_imag = (
        contract(twist_real, sin_inner, second_form) + contract(twist_imag, cos_inner, second_form)
    ) * norm_factor
    return (final_real.reshape(leading + (length,)), final_imag.reshape(leading + (length,)))


def refine_rows(padded, dimension):
    extent = padded.shape[dimension] - 2
    middle = lax.slice_in_dim(padded, 1, extent + 1, axis=dimension)
    previous = lax.slice_in_dim(padded, 0, extent, axis=dimension)
    following = lax.slice_in_dim(padded, 2, extent + 2, axis=dimension)
    pieces = []
    for sub_cell in range(RATIO):
        offset = (sub_cell + 0.5) / RATIO - 0.5
        beside = following if offset > 0 else previous
        pieces.append((1.0 - abs(offset)) * middle + abs(offset) * beside)
    stacked = jnp.stack(pieces, axis=dimension + 1)
    target = list(middle.shape)
    target[dimension] = extent * RATIO
    return stacked.reshape(target)


def spread_table(cell_count):
    fine_count = cell_count * RATIO
    source = lax.broadcasted_iota(jnp.int32, (cell_count + 2, fine_count), 0)
    fine_cell = lax.broadcasted_iota(jnp.int32, (cell_count + 2, fine_count), 1)
    parent = fine_cell // RATIO
    sub_cell = (fine_cell % RATIO).astype(jnp.float32)
    offset = (sub_cell + 0.5) / RATIO - 0.5
    magnitude = jnp.abs(offset)
    own_weight = jnp.where(source == parent + 1, 1.0 - magnitude, 0.0)
    after_weight = jnp.where((source == parent + 2) & (offset > 0), magnitude, 0.0)
    before_weight = jnp.where((source == parent) & (offset < 0), magnitude, 0.0)
    return own_weight + after_weight + before_weight


def average_table(fine_count):
    fine_cell = lax.broadcasted_iota(jnp.int32, (fine_count, fine_count // RATIO), 0)
    coarse_cell = lax.broadcasted_iota(jnp.int32, (fine_count, fine_count // RATIO), 1)
    return jnp.where(fine_cell // RATIO == coarse_cell, 1.0 / RATIO, 0.0).astype(jnp.float32)


def per_device(coarse_modes, salinity, viscosity, forcing_gain, diffusivity):
    planes = coarse_modes.shape[2]
    row_count = coarse_modes.shape[3]
    width = coarse_modes.shape[4]
    groups = lax.axis_size("grp")
    quarter = planes // groups
    pencil = lax.all_to_all(coarse_modes[0], "gx", split_axis=2, concat_axis=3, tiled=True)
    physical = fourier_lines(pencil[0], pencil[1], 1.0, False)
    blocks = lax.all_to_all(physical, "gx", split_axis=2, concat_axis=1, tiled=True)
    received = lax.all_to_all(
        blocks.reshape(groups, quarter, row_count, width),
        "grp",
        split_axis=0,
        concat_axis=0,
        tiled=True,
    )
    rimmed = extended(received, (("gx", 3), ("gy", 2)), 1)
    along_y = refine_rows(rimmed, 2)
    velocity = jnp.einsum(
        "fqyj,jx->fqyx", along_y, spread_table(width), precision=lax.Precision.HIGHEST
    )[:, :, None]
    padded = extended(salinity, (("grp", 0), ("gx", 2), ("gy", 1)), 1)

    def levels(piece):
        return piece.reshape((quarter, RATIO) + piece.shape[1:])

    centre = levels(padded[1:-1, 1:-1, 1:-1])
    east_cells = levels(padded[1:-1, 1:-1, 2:])
    west_cells = levels(padded[1:-1, 1:-1, :-2])
    north_cells = levels(padded[1:-1, 2:, 1:-1])
    south_cells = levels(padded[1:-1, :-2, 1:-1])
    upper_cells = levels(padded[2:, 1:-1, 1:-1])
    lower_cells = levels(padded[:-2, 1:-1, 1:-1])
    diffuse_rate = diffusivity.reshape(quarter, RATIO, 1, 1)
    spread = diffuse_rate * (
        east_cells
        + west_cells
        + north_cells
        + south_cells
        + upper_cells
        + lower_cells
        - 6.0 * centre
    )
    advection = (
        velocity[0] * (east_cells - west_cells) * 0.5
        + velocity[1] * (north_cells - south_cells) * 0.5
        + velocity[2] * (upper_cells - lower_cells) * 0.5
    )
    updated = centre + fine_step * (spread - advection)
    buoyancy = velocity[3] - updated
    partial_mean = buoyancy.reshape(quarter, RATIO, row_count, RATIO, width * RATIO).mean(
        axis=(1, 3)
    )
    restricted = jnp.einsum(
        "qyx,xc->qyc", partial_mean, average_table(width * RATIO), precision=lax.Precision.HIGHEST
    )
    salinity_next = updated.reshape(salinity.shape)
    columns = lax.all_to_all(restricted, "gx", split_axis=1, concat_axis=2, tiled=True)
    spec_real, spec_imag = fourier_lines(columns, None, -1.0, True)
    own_spectra = lax.all_to_all(
        jnp.stack([spec_real, spec_imag]), "gx", split_axis=3, concat_axis=2, tiled=True
    )
    spectrum = lax.all_gather(own_spectra, "grp", axis=1, tiled=True)
    total_modes = width * lax.axis_size("gx")
    mode_index = lax.axis_index("gx") * width + lax.broadcasted_iota(jnp.int32, (width,), 0)
    wavenumber = jnp.where(mode_index < total_modes // 2, mode_index, mode_index - total_modes)
    scaled_wave = 2.0 * math.pi / total_modes * wavenumber.astype(jnp.float32)
    damping = jnp.exp(-viscosity[0] * scaled_wave * scaled_wave)
    coarse_next = damping * coarse_modes + forcing_gain[0] * spectrum[None]
    return (salinity_next, coarse_next)


def solution(mesh):
    return jax.shard_map(
        per_device,
        mesh=mesh,
        in_specs=(
            P("grp", None, None, "gy", "gx"),
            P("grp", "gy", "gx"),
            P("grp"),
            P("grp"),
            P("grp"),
        ),
        out_specs=(P("grp", "gy", "gx"), P("grp", None, None, "gy", "gx")),
        check_vma=False,
    )
```

profile of v0, /device:TPU:0, one launch (start us, length us, event | category | flops | bytes accessed | tf_op | source)
XLA Modules:
  0.0 611.9 jit_solution(15388535690880584705)
XLA Ops:
  21.5 11.6 %copy.106 = f32[8,64,4096]{2,0,1:T(8,128)} copy(f32[8,64,4096]{2,1,0:T(8,128)} %param.6) | data formatting | bytes 16777216 | tf_op args[1]
  33.1 9.9 %reshape.129 = f32[2,4,16,4,4096]{4,3,2,1,0:T(4,128)} reshape(f32[8,64,4096]{2,1,0:T(8,128)} %param.6) | data formatting | bytes 16777216 | tf_op jit(solution)/shard_map/reshape | solution.py:133
  46.1 21.0 %collective-permute-done = f32[1,64,4096]{2,1,0:T(8,128)} collective-permute-done((f32[1,64,4096]{2,1,0:T(8,128)}, f32[1,64,4096]{2,1,0:T(8,128)}, u32[]{:S(2)}, u32[]{:S(2)}) %collective-permute-start) | collective-permute-done | bytes 1048608 | tf_op jit(solution)/shard_map/ppermute | solution.py:18
  78.7 7.5 %copy.128 = f32[8,4,128,32]{0,1,3,2:T(4,128)} copy(f32[8,4,128,32]{2,3,1,0:T(8,128)S(1)} %fusion.39) | data formatting | bytes 1048576 | tf_op jit(solution)/shard_map/reshape | solution.py:66
  86.2 12.1 %reshape.143 = f32[4,1,32768]{2,1,0:T(1,128)} reshape(f32[4096,4,8]{2,1,0:T(4,128)} %bitcast.148) | data formatting | bytes 1048576
  124.4 14.3 %reshape.144 = f32[4096,4,8]{2,1,0:T(4,128)} reshape(f32[4,32768]{1,0:T(4,128)} %reduce) | data formatting | bytes 1048576
  138.7 7.7 %copy.99 = f32[8,4,4,1024]{3,2,1,0:T(4,128)} copy(f32[8,4,4,1024]{0,2,3,1:T(4,128)} %bitcast.149) | data formatting | bytes 1048576 | tf_op jit(solution)/shard_map/all_to_all | solution.py:117
  152.5 8.8 %pad_maximum_fusion.2 = f32[8,64,4096]{2,0,1:T(8,128)} fusion(f32[1,64,4096]{2,0,1:T(1,128)S(1)} %copy.89, f32[8,64,4096]{2,0,1:T(8,128)} %copy.106), kind=kLoop, calls=%fused_computation.38 | loop fusion | flops 2097152 | bytes 17825792 | tf_op jit(solution)/shard_map/concatenate | solution.py:16
  161.3 9.8 %reshape.132 = f32[2,4,16,4,4096]{4,1,0,3,2:T(4,128)} reshape(f32[8,64,4096]{2,0,1:T(8,128)} %pad_maximum_fusion.2) | data formatting | bytes 16777216 | tf_op jit(solution)/shard_map/reshape | solution.py:133
  171.1 21.4 %concatenate.38 = f32[10,64,4098]{2,0,1:T(8,128)} concatenate(f32[10,64,1]{2,0,1:T(8,128)S(1)} %collective-permute-done.3, f32[10,64,4096]{2,0,1:T(8,128)} %copy-done, f32[10,64,1]{2,0,1:T(8,128)S(1)} %collective-permute-done.2), dimensions={2} | concatenate | bytes 20981760 | tf_op jit(solution)/shard_map/concatenate | solution.py:16
  203.5 23.8 %fusion.36 = (f32[8,64,4096]{2,0,1:T(8,128)}, f32[8,64,4096]{2,0,1:T(8,128)}, f32[8,64,4096]{2,0,1:T(8,128)}) fusion(f32[10,64,1]{2,0,1:T(8,128)S(1)} %collective-permute-done.2, f32[1,64,4096]{2,0,1:T(1,128)S(1)} %copy.89, f32[8,64,4096]{2,0,1:T(8,128)} %copy.106, f32[1,64,4096]{2,0,1:T(1,128)S(1)} %copy.87, f32[10,64,1]{2,0,1:T(8,128)S(1)} %collective-permute-done.3), kind=kLoop, calls=%fused_computation.54 | loop fusion | flops 18874368 | bytes 35656704 | tf_op jit(solution)/shard_map/add | solution.py:144
  227.4 9.8 %add.235 = f32[2,4,16,4,4096]{4,1,0,3,2:T(4,128)} reshape(f32[8,64,4096]{2,0,1:T(8,128)} %get-tuple-element.15) | data formatting | bytes 16777216 | tf_op jit(solution)/shard_map/add | solution.py:144
  237.2 9.8 %reshape.133 = f32[2,4,16,4,4096]{4,1,0,3,2:T(4,128)} reshape(f32[8,64,4096]{2,0,1:T(8,128)} %get-tuple-element.17) | data formatting | bytes 16777216 | tf_op jit(solution)/shard_map/reshape | solution.py:133
  247.0 9.8 %sub.118 = f32[2,4,16,4,4096]{4,1,0,3,2:T(4,128)} reshape(f32[8,64,4096]{2,0,1:T(8,128)} %get-tuple-element.16) | data formatting | bytes 16777216 | tf_op jit(solution)/shard_map/sub | solution.py:153
  268.0 43.3 %fusion = f32[4,2,64,4096]{3,2,1,0:T(8,128)} fusion(f32[4,2,64,1026]{3,2,1,0:T(8,128)} %reshape.128, s32[4096]{0:T(1024)S(1)} %copy-done.9, s32[4096]{0:T(1024)} %get-tuple-element.43, s32[4096]{0:T(1024)S(1)} %copy-done.7, s32[4096]{0:T(1024)S(1)} %copy-done.8, pred[4096]{0:T(1024)(128)(4,1)S(1)} %get-tuple-element.45, ...), kind=kOutput, calls=%fused_computation.5 | convolution fusion | flops 25912590336 | bytes 10563584 | tf_op jit(solution)/shard_map/fqyj,jx->fqyx/dot_general | solution.py:127
  311.3 8.4 %fusion.192 = (f32[1,2,64,4096]{3,2,1,0:T(8,128)}, f32[2,64,4096]{2,1,0:T(8,128)S(1)}, f32[2,64,4096]{2,1,0:T(8,128)}, f32[2,64,4096]{2,1,0:T(8,128)}, f32[1,2,6...) fusion(f32[4,2,64,4096]{3,2,1,0:T(8,128)} %fusion), kind=kLoop, calls=%fused_computation.237 | loop fusion | bytes 23068672 | tf_op jit(solution)/shard_map/slice | solution.py:158
  329.6 10.0 %mul.436 = f32[8,64,4096]{2,0,1:T(8,128)} reshape(f32[2,4,64,4096]{3,1,0,2:T(4,128)} %mul.435) | data formatting | bytes 16777216 | tf_op jit(solution)/shard_map/mul | solution.py:153
  344.1 7.0 %mul.439 = f32[2,4,64,4096]{3,1,0,2:T(4,128)} broadcast(f32[2,64,4096]{2,0,1:T(2,128)} %copy.104), dimensions={0,2,3} | broadcast | bytes 10485760 | tf_op jit(solution)/shard_map/mul | solution.py:154
  351.0 10.0 %mul.440 = f32[8,64,4096]{2,0,1:T(8,128)} reshape(f32[2,4,64,4096]{3,1,0,2:T(4,128)} %mul.439) | data formatting | bytes 16777216 | tf_op jit(solution)/shard_map/mul | solution.py:154
  372.6 10.1 %mul.445 = f32[8,64,4096]{2,0,1:T(8,128)} reshape(f32[2,4,64,4096]{3,1,0,2:T(4,128)} %mul.444) | data formatting | bytes 16777216 | tf_op jit(solution)/shard_map/mul | solution.py:155
  382.7 47.6 %multiply_add_fusion.2 = (f32[8,64,4096]{2,0,1:T(8,128)}, f32[8,64,4096]{2,0,1:T(8,128)}, f32[8,64,4096]{2,0,1:T(8,128)}) fusion(f32[8,64,4096]{2,0,1:T(8,128)} %copy.106, f32[8,64,4096]{2,0,1:T(8,128)} %mul.445, f32[8,64,4096]{2,0,1:T(8,128)} %mul.440, f32[8,64,4096]{2,0,1:T(8,128)} %mul.436, f32[8]{0:T(128)S(1)} %copy-done.12, ...), kind=kLoop, calls=%fused_computation.52 | loop fusion | flops 62914560 | bytes 71641280 | tf_op jit(solution)/shard_map/add | solution.py:157
  430.3 9.7 %reshape.130 = f32[2,4,16,4,4096]{4,1,0,3,2:T(4,128)} reshape(f32[8,64,4096]{2,0,1:T(8,128)} %get-tuple-element.10) | data formatting | bytes 16777216 | tf_op jit(solution)/shard_map/reshape | solution.py:133
  440.1 10.0 %reshape.131 = f32[2,4,16,4,4096]{4,1,0,3,2:T(4,128)} reshape(f32[8,64,4096]{2,0,1:T(8,128)} %get-tuple-element.9) | data formatting | bytes 16777216 | tf_op jit(solution)/shard_map/reshape | solution.py:133
  459.8 26.2 %subtract_reduce_fusion = f32[2,16,4096]{2,0,1:T(2,128)S(1)} fusion(f32[2,4,16,4,4096]{4,1,0,3,2:T(4,128)} %reshape.132, f32[2,4,16,4,4096]{4,1,0,3,2:T(4,128)} %reshape.133, f32[2,4,16,4,4096]{4,1,0,3,2:T(4,128)} %reshape.130, f32[2,4,16,4,4096]{4,1,0,3,2:T(4,128)} %reshape.131, f32[2,4,16,4,4096]{4,1,0,3,2:T(4,128)} %sub.118, ...), kind=kLoop, calls=%fused_computation.51 | loop fusion | flops 41811968 | bytes 67633184 | tf_op jit(solution)/shard_map/reduce_sum | solution.py:159
  485.9 11.8 %fusion.15 = f32[2,16,1024]{2,1,0:T(8,128)S(1)} fusion(s32[4096]{0:T(1024)S(1)} %copy-done.7, s32[4096]{0:T(1024)S(1)} %copy-done.8, pred[4096]{0:T(1024)(128)(4,1)S(1)} %get-tuple-element.46, f32[2,16,4096]{2,0,1:T(2,128)S(1)} %subtract_reduce_fusion), kind=kOutput, calls=%fused_computation.20 | convolution fusion | flops 1623326720 | bytes 692224 | tf_op jit(solution)/shard_map/qyx,xc->qyc/dot_general | solution.py:162
  513.6 8.0 %copy.118 = f32[2,2,4,4096]{2,1,0,3:T(2,128)} copy(f32[2,2,4,4096]{3,2,1,0:T(4,128)S(1)} %pad_maximum_fusion.14) | data formatting | bytes 524288 | tf_op jit(solution)/shard_map/stack | solution.py:169
  521.6 14.3 %reshape.145 = f32[4,1,16384]{2,1,0:T(1,128)S(1)} reshape(f32[4096,2,2,4]{3,2,1,0:T(2,128)} %bitcast.150) | data formatting | bytes 524288
  535.9 11.1 %all_to_all.68 = f32[4,1,16384]{2,1,0:T(1,128)S(1)} all-to-all(f32[4,1,16384]{2,1,0:T(1,128)S(1)} %reshape.145), channel_id=1, replica_groups=mesh['grp'=4,'gx'=4,'gy'=2] {'gx'}, dimensions={0} | all-to-all | bytes 524288 | tf_op jit(solution)/shard_map/all_to_all | solution.py:168
  548.4 16.5 %reshape.146 = f32[4096,2,2,4]{3,2,1,0:T(2,128)} reshape(f32[4,16384]{1,0:T(4,128)S(1)} %reduce.1) | data formatting | bytes 524288
  564.9 10.6 %copy.119 = f32[2,2,4,4,1024]{4,3,2,1,0:T(4,128)S(1)} copy(f32[2,2,4,4,1024]{3,1,0,4,2:T(2,128)} %bitcast.151) | data formatting | bytes 524288 | tf_op jit(solution)/shard_map/all_to_all | solution.py:168
  577.6 11.7 %copy.120 = f32[8,64,4096]{2,1,0:T(8,128)} copy(f32[8,64,4096]{2,0,1:T(8,128)} %get-tuple-element.8) | data formatting | bytes 16777216
  589.3 13.1 %all-gather.2.cloned.1.call-done = f32[2,8,16,1024]{3,2,1,0:T(8,128)} async-done(((f32[2,2,16,1024]{3,2,1,0:T(8,128)}), f32[2,8,16,1024]{3,2,1,0:T(8,128)}) %all-gather.2.cloned.1.call-update) | async-done | bytes 1048592 | tf_op jit(solution)/shard_map/all_gather | solution.py:171
  (123 shorter events, 139.1 us)
Async XLA Ops:
  10.0 59.5 %all-to-all-start = ((f32[2,8,16,1024]{3,1,0,2:T(8,128)}), f32[2,8,16,1024]{3,1,0,2:T(8,128)S(1)}, u32[]{:S(2)}, u32[]{:S(2)}) async-start(f32[2,8,16,1024]{3,1,0,2:T(8,128)} %bitcast.143), calls=%async_computation | async-start | bytes 2097152 | tf_op jit(solution)/shard_map/all_to_all | solution.py:115
  19.0 26.0 %collective-permute-start.1 = (f32[1,64,4096]{2,1,0:T(8,128)S(1)}, f32[1,64,4096]{2,1,0:T(8,128)S(1)}, u32[]{:S(2)}, u32[]{:S(2)}) collective-permute-start(f32[1,64,4096]{2,1,0:T(8,128)S(1)} %get-tuple-element.26), channel_id=1, source_target_pairs={{8,0},{16,8},{24,16},{0,24},{9,1},{17,9},{25,17},{1,25},{10,2},{18... | collective-permute-start | bytes 3145736 | tf_op jit(solution)/shard_map/ppermute | solution.py:20
  21.5 45.7 %collective-permute-start = (f32[1,64,4096]{2,1,0:T(8,128)}, f32[1,64,4096]{2,1,0:T(8,128)}, u32[]{:S(2)}, u32[]{:S(2)}) collective-permute-start(f32[1,64,4096]{2,1,0:T(8,128)} %get-tuple-element.25), channel_id=1, source_target_pairs={{0,8},{8,16},{16,24},{24,0},{1,9},{9,17},{17,25},{25,1},{2,10},{10... | collective-permute-start | bytes 3145736 | tf_op jit(solution)/shard_map/ppermute | solution.py:18
  33.1 9.9 %copy-start.11 = (f32[8]{0:T(128)S(1)}, f32[8]{0:T(128)}, u32[]{:S(2)}) copy-start(f32[8]{0:T(128)} %param.9) | copy-start | bytes 100
  43.8 34.0 %copy-start.5 = (f32[32,128]{1,0:T(8,128)}, f32[32,128]{1,0:T(8,128)S(1)}, u32[]{:S(2)}) copy-start(f32[32,128]{1,0:T(8,128)S(1)} %get-tuple-element.40) | copy-start | bytes 49156
  98.3 21.6 %all-to-all-start.1 = ((f32[4,1,32768]{2,1,0:T(1,128)}), f32[4,1,32768]{2,1,0:T(1,128)}, u32[]{:S(2)}, u32[]{:S(2)}) async-start(f32[4,1,32768]{2,1,0:T(1,128)} %reshape.143), calls=%async_computation.1 | async-start | bytes 1048576 | tf_op jit(solution)/shard_map/all_to_all | solution.py:117
  109.2 5.8 copy-start
  116.1 55.0 %collective-permute-start.2 = (f32[10,64,1]{2,0,1:T(8,128)}, f32[10,64,1]{2,0,1:T(8,128)S(1)}, u32[]{:S(2)}, u32[]{:S(2)}) collective-permute-start(f32[10,64,1]{2,0,1:T(8,128)} %get-tuple-element.13), channel_id=1, source_target_pairs={{2,0},{4,2},{6,4},{0,6},{3,1},{5,3},{7,5},{1,7},{10,8},{12,10},{14... | collective-permute-start | bytes 7688 | tf_op jit(solution)/shard_map/ppermute | solution.py:20
  119.9 51.2 %collective-permute-start.3 = (f32[10,64,1]{2,0,1:T(8,128)}, f32[10,64,1]{2,0,1:T(8,128)S(1)}, u32[]{:S(2)}, u32[]{:S(2)}) collective-permute-start(f32[10,64,1]{2,0,1:T(8,128)} %get-tuple-element.14), channel_id=1, source_target_pairs={{0,2},{2,4},{4,6},{6,0},{1,3},{3,5},{5,7},{7,1},{8,10},{10,12},{12... | collective-permute-start | bytes 7688 | tf_op jit(solution)/shard_map/ppermute | solution.py:18
  148.4 44.1 %all-to-all-start.2 = ((f32[4,2,16,1024]{3,2,1,0:T(8,128)}), f32[4,2,16,1024]{3,2,1,0:T(8,128)}, u32[]{:S(2)}, u32[]{:S(2)}) async-start(f32[4,2,16,1024]{3,2,1,0:T(8,128)} %reshape.127), calls=%async_computation.2 | async-start | bytes 1048576 | tf_op jit(solution)/shard_map/all_to_all | solution.py:118
  193.5 6.3 %collective-permute-start.6 = (f32[4,2,16,1]{3,2,1,0:T(8,128)S(1)}, f32[4,2,16,1]{3,2,1,0:T(8,128)S(1)}, u32[]{:S(2)}, u32[]{:S(2)}) collective-permute-start(f32[4,2,16,1]{3,2,1,0:T(8,128)S(1)} %get-tuple-element.38), channel_id=1, source_target_pairs={{0,2},{2,4},{4,6},{6,0},{1,3},{3,5},{5,7},{7,1},{8,10},{10,12},{12... | collective-permute-start | bytes 1544 | tf_op jit(solution)/shard_map/ppermute | solution.py:18
  193.7 6.0 collective-permute-start.7
  199.2 183.4 %collective-permute-start.4 = (f32[10,1,4098]{2,0,1:T(8,128)}, f32[10,1,4098]{2,0,1:T(8,128)S(1)}, u32[]{:S(2)}, u32[]{:S(2)}) collective-permute-start(f32[10,1,4098]{2,0,1:T(8,128)} %get-tuple-element.11), channel_id=1, source_target_pairs={{1,0},{0,1},{3,2},{2,3},{5,4},{4,5},{7,6},{6,7},{9,8},{8,9},{11,10... | collective-permute-start | bytes 491768 | tf_op jit(solution)/shard_map/ppermute | solution.py:20
  199.3 183.5 %collective-permute-start.5 = (f32[10,1,4098]{2,0,1:T(8,128)}, f32[10,1,4098]{2,0,1:T(8,128)}, u32[]{:S(2)}, u32[]{:S(2)}) collective-permute-start(f32[10,1,4098]{2,0,1:T(8,128)} %get-tuple-element.12), channel_id=1, source_target_pairs={{0,1},{1,0},{2,3},{3,2},{4,5},{5,4},{6,7},{7,6},{8,9},{9,8},{10,11... | collective-permute-start | bytes 491768 | tf_op jit(solution)/shard_map/ppermute | solution.py:18
  203.0 53.8 %collective-permute-start.8 = (f32[4,2,1,1026]{3,2,1,0:T(1,128)S(1)}, f32[4,2,1,1026]{3,2,1,0:T(1,128)S(1)}, u32[]{:S(2)}, u32[]{:S(2)}) collective-permute-start(f32[4,2,1,1026]{3,2,1,0:T(1,128)S(1)} %get-tuple-element.35), channel_id=1, source_target_pairs={{0,1},{1,0},{2,3},{3,2},{4,5},{5,4},{6,7},{7,6},{8,9},{9,8},{10,11... | collective-permute-start | bytes 98504 | tf_op jit(solution)/shard_map/ppermute | solution.py:18
  203.0 53.7 %collective-permute-start.9 = (f32[4,2,1,1026]{3,2,1,0:T(1,128)S(1)}, f32[4,2,1,1026]{3,2,1,0:T(1,128)}, u32[]{:S(2)}, u32[]{:S(2)}) collective-permute-start(f32[4,2,1,1026]{3,2,1,0:T(1,128)S(1)} %get-tuple-element.36), channel_id=1, source_target_pairs={{1,0},{0,1},{3,2},{2,3},{5,4},{4,5},{7,6},{6,7},{9,8},{8,9},{11,10... | collective-permute-start | bytes 98504 | tf_op jit(solution)/shard_map/ppermute | solution.py:20
  256.8 11.3 %copy-start.7 = (s32[4096]{0:T(1024)S(1)}, s32[4096]{0:T(1024)}, u32[]{:S(2)}) copy-start(s32[4096]{0:T(1024)} %get-tuple-element.41) | copy-start | bytes 49156
  256.8 11.3 %copy-start.8 = (s32[4096]{0:T(1024)S(1)}, s32[4096]{0:T(1024)}, u32[]{:S(2)}) copy-start(s32[4096]{0:T(1024)} %get-tuple-element.44) | copy-start | bytes 49156
  256.8 11.3 %copy-start.9 = (s32[4096]{0:T(1024)S(1)}, s32[4096]{0:T(1024)}, u32[]{:S(2)}) copy-start(s32[4096]{0:T(1024)} %get-tuple-element.42) | copy-start | bytes 49156
  372.5 10.2 %copy-start.12 = (f32[8]{0:T(128)S(1)}, f32[8]{0:T(128)}, u32[]{:S(2)}) copy-start(f32[8]{0:T(128)} %param.9) | copy-start | bytes 100
  440.1 13.4 %copy-start.3 = (f32[1,2,64,4096]{3,2,1,0:T(8,128)S(1)}, f32[1,2,64,4096]{3,2,1,0:T(8,128)}, u32[]{:S(2)}) copy-start(f32[1,2,64,4096]{3,2,1,0:T(8,128)} %get-tuple-element.24) | copy-start | bytes 6291460
  450.1 5.0 copy-start.2
  450.1 6.7 %copy-start.1 = (f32[1,2,64,4096]{3,2,1,0:T(8,128)S(1)}, f32[1,2,64,4096]{3,2,1,0:T(8,128)}, u32[]{:S(2)}) copy-start(f32[1,2,64,4096]{3,2,1,0:T(8,128)} %get-tuple-element.22) | copy-start | bytes 6291460
  450.1 9.6 %slice-start = ((s8[8388608]{0:T(1024)(128)(4,1)}), s8[4194304]{0:T(1024)(128)(4,1)S(1)}, s32[]{:S(2)}) async-start(s8[8388608]{0:T(1024)(128)(4,1)} %bitcast.146), calls=%async_computation.6 | async-start | bytes 8388608
  450.1 9.6 %copy-start.10 = (f32[2,4]{1,0:T(2,128)S(1)}, f32[2,4]{1,0:T(2,128)}, u32[]{:S(2)}) copy-start(f32[2,4]{1,0:T(2,128)} %mul.460) | copy-start | bytes 100
  455.1 4.6 slice-start.1
  485.9 24.5 %copy-start.6 = (f32[32,128]{1,0:T(8,128)S(1)}, f32[32,128]{1,0:T(8,128)}, u32[]{:S(2)}) copy-start(f32[32,128]{1,0:T(8,128)} %copy-done.5) | copy-start | bytes 49156
  498.5 11.1 %all-to-all-start.3 = ((f32[2,16,1024]{2,0,1:T(2,128)}), f32[2,16,1024]{2,0,1:T(2,128)S(1)}, u32[]{:S(2)}, u32[]{:S(2)}) async-start(f32[2,16,1024]{2,0,1:T(2,128)} %copy.114), calls=%async_computation.3 | async-start | bytes 262144 | tf_op jit(solution)/shard_map/all_to_all | solution.py:166
  503.4 99.0 %all-gather.2.cloned.1.call-start = ((), (), s32[]{:S(2)}) async-start(), calls=%async_computation.5 | async-start | bytes 1310720 | tf_op jit(solution)/shard_map/all_gather | solution.py:171
  577.6 24.9 %copy-start.4 = (f32[1,2,8,16,1024]{4,3,2,1,0:T(8,128)S(1)}, f32[1,2,8,16,1024]{4,3,2,1,0:T(8,128)}, u32[]{:S(2)}) copy-start(f32[1,2,8,16,1024]{4,3,2,1,0:T(8,128)} %param.5) | copy-start | bytes 3145732
Sparse Core Ops, SparseCore 0:
  576.4 26.0 all-gather.1
where the time goes:
time: 621 us; the launch traced here: 612 us
  local copies, waits for them, and re-layouts  322 us (52%)
  other arithmetic  127 us (20%)
  matrix products  63.9 us (10%)
  waiting for transfers between devices  40.1 us (6%)
  starting transfers between devices  32.1 us (5%)
  between operations  16 us (3%)
  blocking collectives  11.1 us (2%)
    unnamed x37, local copies, waits for them, and re-layouts  89.2 us
    reshape x5, local copies, waits for them, and re-layouts, levels(): return piece.reshape((quarter, RATIO) + piece.shape[1:])  49.2 us
    add x1, other arithmetic, per_device(): updated = centre + fine_step * (spread - advection)  47.6 us
    dot_general x1, matrix products, per_device(): jnp.einsum('fqyj,jx->fqyx', along_y, spread_table(width), precision=lax.P...  43.3 us
    reduce_sum x1, other arithmetic, per_device(): buoyancy.reshape(quarter, RATIO, row_count, RATIO, width * RATIO)  26.2 us
    mul x4, local copies, waits for them, and re-layouts, per_device(): velocity[2] * (upper_cells - lower_cells) * 0.5  24.6 us
    add x1, other arithmetic, per_device(): east_cells + west_cells + north_cells + south_cells + upper_cells  23.8 us
    concatenate x2, local copies, waits for them, and re-layouts, extended(): jnp.concatenate([lax.ppermute(tail, axis, [(i, (i + 1) % count) for i in...  23.5 us
  transfers between devices with their start and end apart: 15, of which 3 were waited for; matrix products, arithmetic and copies ran while one was open for 49% of the time, Pallas kernels for 0%

commit v1 on v0

--- a/solution.py
+++ b/solution.py
@@ -3,6 +3,7 @@
 import jax.numpy as jnp
 from jax import lax
 from jax.sharding import PartitionSpec as P
+from jax.lax import all_to_all, axis_size
 
 RATIO = 4
 fine_step = 0.1
@@ -114,7 +115,9 @@
     quarter = planes // groups
     pencil = lax.all_to_all(coarse_modes[0], "gx", split_axis=2, concat_axis=3, tiled=True)
     physical = fourier_lines(pencil[0], pencil[1], 1.0, False)
-    blocks = lax.all_to_all(physical, "gx", split_axis=2, concat_axis=1, tiled=True)
+    blocks = jnp.concatenate(
+        all_to_all(jnp.stack(jnp.split(physical, axis_size("gx"), 2)), "gx", 0, 0), 1
+    )
     received = lax.all_to_all(
         blocks.reshape(groups, quarter, row_count, width),
         "grp",

time: 621 us -> 583 us (0.939)
  local copies, waits for them, and re-layouts: 322 us -> 288 us
    unnamed x37 -> x35, local copies, waits for them, and re-layouts: 89.2 us -> 62.8 us
    all_to_all x2 -> x0, local copies, waits for them, and re-layouts: 8.25 us -> none  [per_device(): lax.all_to_all(physical, 'gx', split_axis=2, concat_axis=1, tiled=True)]
  transfers between devices with their start and end apart: 15 -> 15, of which waited for: 3 -> 3; matrix products, arithmetic and copies ran while one was open for 49% -> 48% of each run, Pallas kernels for 0% -> 0%
where the time goes in v1:
time: 583 us; the launch traced here: 574 us
  local copies, waits for them, and re-layouts  288 us (49%)
  other arithmetic  123 us (21%)
  matrix products  63.7 us (11%)
  waiting for transfers between devices  40.1 us (7%)
  starting transfers between devices  32.2 us (6%)
  between operations  16.2 us (3%)
  blocking collectives  11.1 us (2%)
    unnamed x35, local copies, waits for them, and re-layouts  62.8 us
    reshape x5, local copies, waits for them, and re-layouts, levels(): return piece.reshape((quarter, RATIO) + piece.shape[1:])  49.3 us
    add x1, other arithmetic, per_device(): updated = centre + fine_step * (spread - advection)  47.7 us
    dot_general x1, matrix products, per_device(): jnp.einsum('fqyj,jx->fqyx', along_y, spread_table(width), precision=lax.P...  43.1 us
    reduce_sum x1, other arithmetic, per_device(): buoyancy.reshape(quarter, RATIO, row_count, RATIO, width * RATIO)  25.9 us
    mul x4, local copies, waits for them, and re-layouts, per_device(): velocity[2] * (upper_cells - lower_cells) * 0.5  24.8 us
    add x1, other arithmetic, per_device(): east_cells + west_cells + north_cells + south_cells + upper_cells  23.7 us
    concatenate x2, local copies, waits for them, and re-layouts, extended(): jnp.concatenate([lax.ppermute(tail, axis, [(i, (i + 1) % count) for i in...  23.5 us
  transfers between devices with their start and end apart: 15, of which 3 were waited for; matrix products, arithmetic and copies ran while one was open for 48% of the time, Pallas kernels for 0%

profile of v1, /device:TPU:0, one launch (start us, length us, event | category | flops | bytes accessed | tf_op | source)
XLA Modules:
  0.0 574.0 jit_solution(10951191359580573830)
XLA Ops:
  10.0 6.3 %all-to-all-start = ((f32[2,8,16,1024]{3,1,0,2:T(8,128)}), f32[2,8,16,1024]{3,1,0,2:T(8,128)S(1)}, u32[]{:S(2)}, u32[]{:S(2)}) async-start(f32[2,8,16,1024]{3,1,0,2:T(8,128)} %bitcast.154), calls=%async_computation | async-start | bytes 2097152 | tf_op jit(solution)/shard_map/all_to_all | solution.py:116
  21.5 11.6 %copy.106 = f32[8,64,4096]{2,0,1:T(8,128)} copy(f32[8,64,4096]{2,1,0:T(8,128)} %param.6) | data formatting | bytes 16777216 | tf_op args[1]
  33.1 10.0 %reshape.128 = f32[2,4,16,4,4096]{4,3,2,1,0:T(4,128)} reshape(f32[8,64,4096]{2,1,0:T(8,128)} %param.6) | data formatting | bytes 16777216 | tf_op jit(solution)/shard_map/reshape | solution.py:136
  46.2 21.0 %collective-permute-done = f32[1,64,4096]{2,1,0:T(8,128)} collective-permute-done((f32[1,64,4096]{2,1,0:T(8,128)}, f32[1,64,4096]{2,1,0:T(8,128)}, u32[]{:S(2)}, u32[]{:S(2)}) %collective-permute-start) | collective-permute-done | bytes 1048608 | tf_op jit(solution)/shard_map/ppermute | solution.py:19
  114.2 8.8 %pad_maximum_fusion.2 = f32[8,64,4096]{2,0,1:T(8,128)} fusion(f32[1,64,4096]{2,0,1:T(1,128)S(1)} %copy.90, f32[8,64,4096]{2,0,1:T(8,128)} %copy.106), kind=kLoop, calls=%fused_computation.38 | loop fusion | flops 2097152 | bytes 17825792 | tf_op jit(solution)/shard_map/concatenate | solution.py:17
  122.9 9.8 %reshape.131 = f32[2,4,16,4,4096]{4,1,0,3,2:T(4,128)} reshape(f32[8,64,4096]{2,0,1:T(8,128)} %pad_maximum_fusion.2) | data formatting | bytes 16777216 | tf_op jit(solution)/shard_map/reshape | solution.py:136
  132.7 21.5 %concatenate.38 = f32[10,64,4098]{2,0,1:T(8,128)} concatenate(f32[10,64,1]{2,0,1:T(8,128)S(1)} %collective-permute-done.3, f32[10,64,4096]{2,0,1:T(8,128)} %copy-done, f32[10,64,1]{2,0,1:T(8,128)S(1)} %collective-permute-done.2), dimensions={2} | concatenate | bytes 20981760 | tf_op jit(solution)/shard_map/concatenate | solution.py:17
  165.2 23.7 %fusion.36 = (f32[8,64,4096]{2,0,1:T(8,128)}, f32[8,64,4096]{2,0,1:T(8,128)}, f32[8,64,4096]{2,0,1:T(8,128)}) fusion(f32[10,64,1]{2,0,1:T(8,128)S(1)} %collective-permute-done.2, f32[1,64,4096]{2,0,1:T(1,128)S(1)} %copy.90, f32[8,64,4096]{2,0,1:T(8,128)} %copy.106, f32[1,64,4096]{2,0,1:T(1,128)S(1)} %copy.88, f32[10,64,1]{2,0,1:T(8,128)S(1)} %collective-permute-done.3), kind=kLoop, calls=%fused_computation.54 | loop fusion | flops 18874368 | bytes 35656704 | tf_op jit(solution)/shard_map/add | solution.py:147
  188.9 9.9 %add.235 = f32[2,4,16,4,4096]{4,1,0,3,2:T(4,128)} reshape(f32[8,64,4096]{2,0,1:T(8,128)} %get-tuple-element.15) | data formatting | bytes 16777216 | tf_op jit(solution)/shard_map/add | solution.py:147
  198.8 9.8 %reshape.132 = f32[2,4,16,4,4096]{4,1,0,3,2:T(4,128)} reshape(f32[8,64,4096]{2,0,1:T(8,128)} %get-tuple-element.17) | data formatting | bytes 16777216 | tf_op jit(solution)/shard_map/reshape | solution.py:136
  208.5 9.8 %sub.118 = f32[2,4,16,4,4096]{4,1,0,3,2:T(4,128)} reshape(f32[8,64,4096]{2,0,1:T(8,128)} %get-tuple-element.16) | data formatting | bytes 16777216 | tf_op jit(solution)/shard_map/sub | solution.py:156
  229.6 43.1 %fusion = f32[4,2,64,4096]{3,2,1,0:T(8,128)} fusion(f32[4,2,64,1026]{3,2,1,0:T(8,128)} %reshape.127, s32[4096]{0:T(1024)S(1)} %copy-done.9, s32[4096]{0:T(1024)} %get-tuple-element.47, s32[4096]{0:T(1024)S(1)} %copy-done.7, s32[4096]{0:T(1024)S(1)} %copy-done.8, pred[4096]{0:T(1024)(128)(4,1)S(1)} %get-tuple-element.49, ...), kind=kOutput, calls=%fused_computation.5 | convolution fusion | flops 25912590336 | bytes 10563584 | tf_op jit(solution)/shard_map/fqyj,jx->fqyx/dot_general | solution.py:130
  272.6 8.4 %fusion.192 = (f32[1,2,64,4096]{3,2,1,0:T(8,128)}, f32[2,64,4096]{2,1,0:T(8,128)S(1)}, f32[2,64,4096]{2,1,0:T(8,128)}, f32[2,64,4096]{2,1,0:T(8,128)}, f32[1,2,6...) fusion(f32[4,2,64,4096]{3,2,1,0:T(8,128)} %fusion), kind=kLoop, calls=%fused_computation.242 | loop fusion | bytes 23068672 | tf_op jit(solution)/shard_map/slice | solution.py:161
  284.0 7.0 %mul.435 = f32[2,4,64,4096]{3,1,0,2:T(4,128)} broadcast(f32[2,64,4096]{2,0,1:T(2,128)} %copy.103), dimensions={0,2,3} | broadcast | bytes 10485760 | tf_op jit(solution)/shard_map/mul | solution.py:156
  290.9 10.0 %mul.436 = f32[8,64,4096]{2,0,1:T(8,128)} reshape(f32[2,4,64,4096]{3,1,0,2:T(4,128)} %mul.435) | data formatting | bytes 16777216 | tf_op jit(solution)/shard_map/mul | solution.py:156
  305.4 7.0 %mul.439 = f32[2,4,64,4096]{3,1,0,2:T(4,128)} broadcast(f32[2,64,4096]{2,0,1:T(2,128)} %copy.104), dimensions={0,2,3} | broadcast | bytes 10485760 | tf_op jit(solution)/shard_map/mul | solution.py:157
  312.4 10.0 %mul.440 = f32[8,64,4096]{2,0,1:T(8,128)} reshape(f32[2,4,64,4096]{3,1,0,2:T(4,128)} %mul.439) | data formatting | bytes 16777216 | tf_op jit(solution)/shard_map/mul | solution.py:157
  327.0 7.0 %mul.444 = f32[2,4,64,4096]{3,1,0,2:T(4,128)} broadcast(f32[2,64,4096]{2,0,1:T(2,128)} %copy.105), dimensions={0,2,3} | broadcast | bytes 10485760 | tf_op jit(solution)/shard_map/mul | solution.py:158
  333.9 10.4 %mul.445 = f32[8,64,4096]{2,0,1:T(8,128)} reshape(f32[2,4,64,4096]{3,1,0,2:T(4,128)} %mul.444) | data formatting | bytes 16777216 | tf_op jit(solution)/shard_map/mul | solution.py:158
  344.3 47.7 %multiply_add_fusion.2 = (f32[8,64,4096]{2,0,1:T(8,128)}, f32[8,64,4096]{2,0,1:T(8,128)}, f32[8,64,4096]{2,0,1:T(8,128)}) fusion(f32[8,64,4096]{2,0,1:T(8,128)} %copy.106, f32[8,64,4096]{2,0,1:T(8,128)} %mul.445, f32[8,64,4096]{2,0,1:T(8,128)} %mul.440, f32[8,64,4096]{2,0,1:T(8,128)} %mul.436, f32[8]{0:T(128)S(1)} %copy-done.12, ...), kind=kLoop, calls=%fused_computation.52 | loop fusion | flops 62914560 | bytes 71641280 | tf_op jit(solution)/shard_map/add | solution.py:160
  392.0 9.7 %reshape.129 = f32[2,4,16,4,4096]{4,1,0,3,2:T(4,128)} reshape(f32[8,64,4096]{2,0,1:T(8,128)} %get-tuple-element.10) | data formatting | bytes 16777216 | tf_op jit(solution)/shard_map/reshape | solution.py:136
  401.7 10.0 %reshape.130 = f32[2,4,16,4,4096]{4,1,0,3,2:T(4,128)} reshape(f32[8,64,4096]{2,0,1:T(8,128)} %get-tuple-element.9) | data formatting | bytes 16777216 | tf_op jit(solution)/shard_map/reshape | solution.py:136
  421.3 25.9 %subtract_reduce_fusion = f32[2,16,4096]{2,0,1:T(2,128)S(1)} fusion(f32[2,4,16,4,4096]{4,1,0,3,2:T(4,128)} %reshape.131, f32[2,4,16,4,4096]{4,1,0,3,2:T(4,128)} %reshape.132, f32[2,4,16,4,4096]{4,1,0,3,2:T(4,128)} %reshape.129, f32[2,4,16,4,4096]{4,1,0,3,2:T(4,128)} %reshape.130, f32[2,4,16,4,4096]{4,1,0,3,2:T(4,128)} %sub.118, ...), kind=kLoop, calls=%fused_computation.51 | loop fusion | flops 41811968 | bytes 67633184 | tf_op jit(solution)/shard_map/reduce_sum | solution.py:162
  447.3 11.8 %fusion.15 = f32[2,16,1024]{2,1,0:T(8,128)S(1)} fusion(s32[4096]{0:T(1024)S(1)} %copy-done.7, s32[4096]{0:T(1024)S(1)} %copy-done.8, pred[4096]{0:T(1024)(128)(4,1)S(1)} %get-tuple-element.50, f32[2,16,4096]{2,0,1:T(2,128)S(1)} %subtract_reduce_fusion), kind=kOutput, calls=%fused_computation.20 | convolution fusion | flops 1623326720 | bytes 692224 | tf_op jit(solution)/shard_map/qyx,xc->qyc/dot_general | solution.py:165
  465.1 5.8 %all-to-all-done.3 = f32[2,16,1024]{2,0,1:T(2,128)S(1)} async-done(((f32[2,16,1024]{2,0,1:T(2,128)}), f32[2,16,1024]{2,0,1:T(2,128)S(1)}, u32[]{:S(2)}, u32[]{:S(2)}) %all-to-all-start.3) | async-done | bytes 131104 | tf_op jit(solution)/shard_map/all_to_all | solution.py:169
  474.9 8.0 %copy.118 = f32[2,2,4,4096]{2,1,0,3:T(2,128)} copy(f32[2,2,4,4096]{3,2,1,0:T(4,128)S(1)} %pad_maximum_fusion.15) | data formatting | bytes 524288 | tf_op jit(solution)/shard_map/stack | solution.py:172
  482.9 14.3 %reshape.142 = f32[4,1,16384]{2,1,0:T(1,128)S(1)} reshape(f32[4096,2,2,4]{3,2,1,0:T(2,128)} %bitcast.159) | data formatting | bytes 524288
  497.2 11.1 %all_to_all.58 = f32[4,1,16384]{2,1,0:T(1,128)S(1)} all-to-all(f32[4,1,16384]{2,1,0:T(1,128)S(1)} %reshape.142), channel_id=1, replica_groups=mesh['grp'=4,'gx'=4,'gy'=2] {'gx'}, dimensions={0} | all-to-all | bytes 524288 | tf_op jit(solution)/shard_map/all_to_all | solution.py:171
  510.2 16.5 %reshape.143 = f32[4096,2,2,4]{3,2,1,0:T(2,128)} reshape(f32[4,16384]{1,0:T(4,128)S(1)} %reduce) | data formatting | bytes 524288
  526.7 10.6 %copy.119 = f32[2,2,4,4,1024]{4,3,2,1,0:T(4,128)S(1)} copy(f32[2,2,4,4,1024]{3,1,0,4,2:T(2,128)} %bitcast.160) | data formatting | bytes 524288 | tf_op jit(solution)/shard_map/all_to_all | solution.py:171
  539.5 11.7 %copy.120 = f32[8,64,4096]{2,1,0:T(8,128)} copy(f32[8,64,4096]{2,0,1:T(8,128)} %get-tuple-element.8) | data formatting | bytes 16777216
  551.2 13.2 %all-gather.2.cloned.1.call-done = f32[2,8,16,1024]{3,2,1,0:T(8,128)} async-done(((f32[2,2,16,1024]{3,2,1,0:T(8,128)}), f32[2,8,16,1024]{3,2,1,0:T(8,128)}) %all-gather.2.cloned.1.call-update) | async-done | bytes 1048592 | tf_op jit(solution)/shard_map/all_gather | solution.py:174
  (123 shorter events, 116.7 us)
Async XLA Ops:
  10.0 59.5 %all-to-all-start = ((f32[2,8,16,1024]{3,1,0,2:T(8,128)}), f32[2,8,16,1024]{3,1,0,2:T(8,128)S(1)}, u32[]{:S(2)}, u32[]{:S(2)}) async-start(f32[2,8,16,1024]{3,1,0,2:T(8,128)} %bitcast.154), calls=%async_computation | async-start | bytes 2097152 | tf_op jit(solution)/shard_map/all_to_all | solution.py:116
  19.1 26.1 %collective-permute-start.1 = (f32[1,64,4096]{2,1,0:T(8,128)S(1)}, f32[1,64,4096]{2,1,0:T(8,128)S(1)}, u32[]{:S(2)}, u32[]{:S(2)}) collective-permute-start(f32[1,64,4096]{2,1,0:T(8,128)S(1)} %get-tuple-element.26), channel_id=1, source_target_pairs={{8,0},{16,8},{24,16},{0,24},{9,1},{17,9},{25,17},{1,25},{10,2},{18... | collective-permute-start | bytes 3145736 | tf_op jit(solution)/shard_map/ppermute | solution.py:21
  21.5 45.7 %collective-permute-start = (f32[1,64,4096]{2,1,0:T(8,128)}, f32[1,64,4096]{2,1,0:T(8,128)}, u32[]{:S(2)}, u32[]{:S(2)}) collective-permute-start(f32[1,64,4096]{2,1,0:T(8,128)} %get-tuple-element.25), channel_id=1, source_target_pairs={{0,8},{8,16},{16,24},{24,0},{1,9},{9,17},{17,25},{25,1},{2,10},{10... | collective-permute-start | bytes 3145736 | tf_op jit(solution)/shard_map/ppermute | solution.py:19
  33.1 10.0 %copy-start.11 = (f32[8]{0:T(128)S(1)}, f32[8]{0:T(128)}, u32[]{:S(2)}) copy-start(f32[8]{0:T(128)} %param.9) | copy-start | bytes 100
  43.9 34.0 %copy-start.5 = (f32[32,128]{1,0:T(8,128)}, f32[32,128]{1,0:T(8,128)S(1)}, u32[]{:S(2)}) copy-start(f32[32,128]{1,0:T(8,128)S(1)} %get-tuple-element.44) | copy-start | bytes 49156
  84.1 21.2 %all-to-all-start.1 = ((f32[4,8,4,1024]{3,1,2,0:T(8,128)}), f32[4,8,4,1024]{3,1,2,0:T(8,128)}, u32[]{:S(2)}, u32[]{:S(2)}) async-start(f32[4,8,4,1024]{3,1,2,0:T(8,128)} %pad_maximum_fusion.14), calls=%async_computation.1 | async-start | bytes 1048576 | tf_op jit(solution)/shard_map/all_to_all | solution.py:119
  94.5 5.8 %copy-start = (f32[10,64,4096]{2,0,1:T(8,128)}, f32[10,64,4096]{2,0,1:T(8,128)S(1)}, u32[]{:S(2)}) copy-start(f32[10,64,4096]{2,0,1:T(8,128)S(1)} %pad_maximum_fusion) | copy-start | bytes 31457284
  101.4 31.3 %collective-permute-start.2 = (f32[10,64,1]{2,0,1:T(8,128)}, f32[10,64,1]{2,0,1:T(8,128)S(1)}, u32[]{:S(2)}, u32[]{:S(2)}) collective-permute-start(f32[10,64,1]{2,0,1:T(8,128)} %get-tuple-element.13), channel_id=1, source_target_pairs={{2,0},{4,2},{6,4},{0,6},{3,1},{5,3},{7,5},{1,7},{10,8},{12,10},{14... | collective-permute-start | bytes 7688 | tf_op jit(solution)/shard_map/ppermute | solution.py:21
  105.3 27.4 %collective-permute-start.3 = (f32[10,64,1]{2,0,1:T(8,128)}, f32[10,64,1]{2,0,1:T(8,128)S(1)}, u32[]{:S(2)}, u32[]{:S(2)}) collective-permute-start(f32[10,64,1]{2,0,1:T(8,128)} %get-tuple-element.14), channel_id=1, source_target_pairs={{0,2},{2,4},{4,6},{6,0},{1,3},{3,5},{5,7},{7,1},{8,10},{10,12},{12... | collective-permute-start | bytes 7688 | tf_op jit(solution)/shard_map/ppermute | solution.py:19
  109.5 44.6 %all-to-all-start.2 = ((f32[4,2,16,1024]{3,2,1,0:T(8,128)}), f32[4,2,16,1024]{3,2,1,0:T(8,128)}, u32[]{:S(2)}, u32[]{:S(2)}) async-start(f32[4,2,16,1024]{3,2,1,0:T(8,128)} %copy.99), calls=%async_computation.2 | async-start | bytes 1048576 | tf_op jit(solution)/shard_map/all_to_all | solution.py:121
  155.1 6.3 %collective-permute-start.6 = (f32[4,2,16,1]{3,2,1,0:T(8,128)S(1)}, f32[4,2,16,1]{3,2,1,0:T(8,128)S(1)}, u32[]{:S(2)}, u32[]{:S(2)}) collective-permute-start(f32[4,2,16,1]{3,2,1,0:T(8,128)S(1)} %get-tuple-element.38), channel_id=1, source_target_pairs={{0,2},{2,4},{4,6},{6,0},{1,3},{3,5},{5,7},{7,1},{8,10},{10,12},{12... | collective-permute-start | bytes 1544 | tf_op jit(solution)/shard_map/ppermute | solution.py:19
  155.4 6.0 %collective-permute-start.7 = (f32[4,2,16,1]{3,2,1,0:T(8,128)S(1)}, f32[4,2,16,1]{3,2,1,0:T(8,128)S(1)}, u32[]{:S(2)}, u32[]{:S(2)}) collective-permute-start(f32[4,2,16,1]{3,2,1,0:T(8,128)S(1)} %get-tuple-element.37), channel_id=1, source_target_pairs={{2,0},{4,2},{6,4},{0,6},{3,1},{5,3},{7,5},{1,7},{10,8},{12,10},{14... | collective-permute-start | bytes 1544 | tf_op jit(solution)/shard_map/ppermute | solution.py:21
  160.9 183.4 %collective-permute-start.4 = (f32[10,1,4098]{2,0,1:T(8,128)}, f32[10,1,4098]{2,0,1:T(8,128)S(1)}, u32[]{:S(2)}, u32[]{:S(2)}) collective-permute-start(f32[10,1,4098]{2,0,1:T(8,128)} %get-tuple-element.11), channel_id=1, source_target_pairs={{1,0},{0,1},{3,2},{2,3},{5,4},{4,5},{7,6},{6,7},{9,8},{8,9},{11,10... | collective-permute-start | bytes 491768 | tf_op jit(solution)/shard_map/ppermute | solution.py:21
  160.9 183.4 %collective-permute-start.5 = (f32[10,1,4098]{2,0,1:T(8,128)}, f32[10,1,4098]{2,0,1:T(8,128)}, u32[]{:S(2)}, u32[]{:S(2)}) collective-permute-start(f32[10,1,4098]{2,0,1:T(8,128)} %get-tuple-element.12), channel_id=1, source_target_pairs={{0,1},{1,0},{2,3},{3,2},{4,5},{5,4},{6,7},{7,6},{8,9},{9,8},{10,11... | collective-permute-start | bytes 491768 | tf_op jit(solution)/shard_map/ppermute | solution.py:19
  164.6 53.7 %collective-permute-start.8 = (f32[4,2,1,1026]{3,2,1,0:T(1,128)S(1)}, f32[4,2,1,1026]{3,2,1,0:T(1,128)S(1)}, u32[]{:S(2)}, u32[]{:S(2)}) collective-permute-start(f32[4,2,1,1026]{3,2,1,0:T(1,128)S(1)} %get-tuple-element.35), channel_id=1, source_target_pairs={{0,1},{1,0},{2,3},{3,2},{4,5},{5,4},{6,7},{7,6},{8,9},{9,8},{10,11... | collective-permute-start | bytes 98504 | tf_op jit(solution)/shard_map/ppermute | solution.py:19
  164.7 53.6 %collective-permute-start.9 = (f32[4,2,1,1026]{3,2,1,0:T(1,128)S(1)}, f32[4,2,1,1026]{3,2,1,0:T(1,128)}, u32[]{:S(2)}, u32[]{:S(2)}) collective-permute-start(f32[4,2,1,1026]{3,2,1,0:T(1,128)S(1)} %get-tuple-element.36), channel_id=1, source_target_pairs={{1,0},{0,1},{3,2},{2,3},{5,4},{4,5},{7,6},{6,7},{9,8},{8,9},{11,10... | collective-permute-start | bytes 98504 | tf_op jit(solution)/shard_map/ppermute | solution.py:21
  218.3 11.3 %copy-start.7 = (s32[4096]{0:T(1024)S(1)}, s32[4096]{0:T(1024)}, u32[]{:S(2)}) copy-start(s32[4096]{0:T(1024)} %get-tuple-element.45) | copy-start | bytes 49156
  218.3 11.2 %copy-start.8 = (s32[4096]{0:T(1024)S(1)}, s32[4096]{0:T(1024)}, u32[]{:S(2)}) copy-start(s32[4096]{0:T(1024)} %get-tuple-element.48) | copy-start | bytes 49156
  218.3 11.2 %copy-start.9 = (s32[4096]{0:T(1024)S(1)}, s32[4096]{0:T(1024)}, u32[]{:S(2)}) copy-start(s32[4096]{0:T(1024)} %get-tuple-element.46) | copy-start | bytes 49156
  333.9 10.4 %copy-start.12 = (f32[8]{0:T(128)S(1)}, f32[8]{0:T(128)}, u32[]{:S(2)}) copy-start(f32[8]{0:T(128)} %param.9) | copy-start | bytes 100
  401.7 13.4 %copy-start.3 = (f32[1,2,64,4096]{3,2,1,0:T(8,128)S(1)}, f32[1,2,64,4096]{3,2,1,0:T(8,128)}, u32[]{:S(2)}) copy-start(f32[1,2,64,4096]{3,2,1,0:T(8,128)} %get-tuple-element.24) | copy-start | bytes 6291460
  411.7 5.0 copy-start.2
  411.7 6.7 %copy-start.1 = (f32[1,2,64,4096]{3,2,1,0:T(8,128)S(1)}, f32[1,2,64,4096]{3,2,1,0:T(8,128)}, u32[]{:S(2)}) copy-start(f32[1,2,64,4096]{3,2,1,0:T(8,128)} %get-tuple-element.22) | copy-start | bytes 6291460
  411.7 9.6 %slice-start = ((s8[8388608]{0:T(1024)(128)(4,1)}), s8[4194304]{0:T(1024)(128)(4,1)S(1)}, s32[]{:S(2)}) async-start(s8[8388608]{0:T(1024)(128)(4,1)} %bitcast.157), calls=%async_computation.6 | async-start | bytes 8388608
  411.7 9.6 %copy-start.10 = (f32[2,4]{1,0:T(2,128)S(1)}, f32[2,4]{1,0:T(2,128)}, u32[]{:S(2)}) copy-start(f32[2,4]{1,0:T(2,128)} %mul.460) | copy-start | bytes 100
  416.7 4.6 slice-start.1
  447.3 24.5 %copy-start.6 = (f32[32,128]{1,0:T(8,128)S(1)}, f32[32,128]{1,0:T(8,128)}, u32[]{:S(2)}) copy-start(f32[32,128]{1,0:T(8,128)} %copy-done.5) | copy-start | bytes 49156
  459.8 11.1 %all-to-all-start.3 = ((f32[2,16,1024]{2,0,1:T(2,128)}), f32[2,16,1024]{2,0,1:T(2,128)S(1)}, u32[]{:S(2)}, u32[]{:S(2)}) async-start(f32[2,16,1024]{2,0,1:T(2,128)} %copy.114), calls=%async_computation.3 | async-start | bytes 262144 | tf_op jit(solution)/shard_map/all_to_all | solution.py:169
  464.8 99.6 %all-gather.2.cloned.1.call-start = ((), (), s32[]{:S(2)}) async-start(), calls=%async_computation.5 | async-start | bytes 1310720 | tf_op jit(solution)/shard_map/all_gather | solution.py:174
  539.4 24.9 %copy-start.4 = (f32[1,2,8,16,1024]{4,3,2,1,0:T(8,128)S(1)}, f32[1,2,8,16,1024]{4,3,2,1,0:T(8,128)}, u32[]{:S(2)}) copy-start(f32[1,2,8,16,1024]{4,3,2,1,0:T(8,128)} %param.5) | copy-start | bytes 3145732
Sparse Core Ops, SparseCore 0:
  538.3 26.0 all-gather.1
